TPU v7x, 32 devices: a whole 2x2x4 slice. The times are simulated.
32 devices in a mesh: seq: 8 (over z, y), head: 4 (over x, core).
Axes of the slice: x: 2, y: 2, z: 4, core: 2. Of those that a mesh axis runs over, the one named last changes fastest.
Arguments:
- tokens: bfloat16 [8192, 2048], P('seq'), may hold values from -6 to 6
- w_query: bfloat16 [2048, 2048], P(None, 'head'), may hold values from -0.125 to 0.125
- w_key: bfloat16 [2048, 2048], P(None, 'head'), may hold values from -0.125 to 0.125
- w_value: bfloat16 [2048, 2048], P(None, 'head'), may hold values from -0.125 to 0.125
- w_out: bfloat16 [2048, 2048], P('head'), may hold values from -0.125 to 0.125
- norm_gain: float32 [2048], P('head'), may hold values from 0.5 to 1.5
- forget_rate: float32 [8192, 16], P('seq', 'head'), may hold values from 0 to 2, as said below
- routing: int32 [128, 16, 2], P('seq', 'head'), may hold values from 0 to 7, all different within a row
- memory_blend_share: float32 [128, 16, 2], P('seq', 'head'), may hold values from 0.25 to 1
Outputs:
- mixed: bfloat16 [8192, 2048], P(('seq', 'head'))
Inputs may be any that keep to these rules, and one draw needn't show every extreme that they name: `routing`: each block and head names 2 different memories. `forget_rate`: positive rates.
All inputs are finite; a program needn't handle non-finite values.
Results may differ from a plain program's by a relative error of at most 0.03.
Values may be sent and summed in bfloat16 or wider, within the bound.
A program may use at most 128 MiB of HBM per device.

v0:
```python
import jax
import jax.numpy as jnp
from jax import lax
from jax.experimental import pallas as pl
from jax.experimental.pallas import tpu as pltpu
from jax.sharding import PartitionSpec as P

HD = 128
M = 8
CH = 64

HIGH = lax.Precision.HIGHEST
MESH = pl.DeviceIdType.MESH
VMEM = pltpu.VMEM
SMEM = pltpu.SMEM
PARTS = 4
LIMIT = 60 * 1024 * 1024


def local_kernel(
    chosen,
    shares,
    k_ref,
    v_ref,
    rate_ref,
    key_ref,
    state_ref,
    mem_ref,
    column_ref,
    line_ref,
    entry_ref,
    prod_ref,
):
    tok_rows, local_heads = rate_ref.shape
    blocks = tok_rows // CH
    mem_ref[...] = jnp.zeros_like(mem_ref)
    prod_ref[...] = jnp.ones_like(prod_ref)
    t = lax.broadcasted_iota(jnp.int32, (CH, CH), 0)
    s = lax.broadcasted_iota(jnp.int32, (CH, CH), 1)

    def block(b, carry):
        rows = pl.ds(pl.multiple_of(b * CH, CH), CH)
        rates = rate_ref[rows, :]
        columns = -jnp.dot(
            jnp.where(t >= s, 1.0, 0.0), rates, precision=HIGH, preferred_element_type=jnp.float32
        )
        lines = -lax.dot_general(
            rates,
            jnp.where(t <= s, 1.0, 0.0),
            (((0,), (0,)), ((), ())),
            precision=HIGH,
            preferred_element_type=jnp.float32,
        )
        growths = jnp.exp(columns)
        column_ref[rows, :] = columns
        line_ref[b] = lines
        for h in range(local_heads):
            cols = slice(h * HD, (h + 1) * HD)
            wide = k_ref[rows, cols].astype(jnp.float32)
            values = v_ref[rows, cols]
            keys = wide * lax.rsqrt(jnp.sum(wide * wide, axis=-1, keepdims=True) + 1e-06)
            keys = keys.astype(jnp.bfloat16)
            key_ref[rows, cols] = keys
            column = columns[:, h : h + 1]
            ending = column[CH - 1 : CH]
            scaled = (keys.astype(jnp.float32) * jnp.exp(ending - column)).astype(jnp.bfloat16)
            written = lax.dot_general(
                scaled, values, (((0,), (0,)), ((), ())), preferred_element_type=jnp.float32
            )
            at = (b * local_heads + h) * 2
            first, second = h * M + chosen[at], h * M + chosen[at + 1]
            share_a, share_b = shares[at], shares[at + 1]
            fade = jnp.broadcast_to(growths[CH - 1 : CH, h : h + 1], (1, HD))
            old_a = mem_ref[first]
            old_b = mem_ref[second]
            state_ref[b * local_heads + h] = (share_a * old_a + share_b * old_b).astype(jnp.bfloat16)
            mem_ref[first] = fade * old_a + written
            mem_ref[second] = fade * old_b + written
            prod_a, prod_b = prod_ref[first], prod_ref[second]
            entry_ref[at] = share_a * prod_a
            entry_ref[at + 1] = share_b * prod_b
            prod_ref[first] = fade * prod_a
            prod_ref[second] = fade * prod_b
        return carry

    lax.fori_loop(0, blocks, block, 0, unroll=4)


def weights_of(owner, depth):
    return pl.ds(pl.multiple_of(owner * depth, depth), depth)


def chain_kernel(
    chosen,
    shares,
    entry_ref,
    prod_ref,
    mem_ref,
    q_ref,
    key_ref,
    v_ref,
    column_ref,
    line_ref,
    state_ref,
    gain_ref,
    w_ref,
    exchanged,
    gathered,
    inbox,
    outbox,
    current,
    finished,
    send_sem,
    recv_sem,
    row_send,
    row_recv,
    own_sem,
    near_send,
    near_recv,
    pass_send,
    pass_recv,
):
    size, me = lax.axis_size("seq"), lax.axis_index("seq")
    groups, mine = lax.axis_size("head"), lax.axis_index("head")
    pieces = mem_ref.shape[0]
    local_heads = pieces // M
    width = local_heads * HD
    blocks = q_ref.shape[0] // CH
    own_rows = q_ref.shape[0] // groups
    barrier = pltpu.get_barrier_semaphore()

    @pl.when(me > 0)
    def _():
        pl.semaphore_signal(barrier, 1, device_id={"seq": me - 1}, device_id_type=MESH)

    @pl.when(me < size - 1)
    def _():
        pl.semaphore_signal(barrier, 1, device_id={"seq": me + 1}, device_id_type=MESH)

    for k in range(1, groups):
        pl.semaphore_signal(
            barrier, 1, device_id={"head": lax.rem(mine + k, groups)}, device_id_type=MESH
        )
    peers = jnp.where(me > 0, 1, 0) + jnp.where(me < size - 1, 1, 0) + (groups - 1)
    pl.semaphore_wait(barrier, peers)

    @pl.when(me == 0)
    def _():
        inbox[...] = jnp.zeros_like(inbox)

    def copy(c):
        return pltpu.make_async_remote_copy(
            src_ref=outbox.at[c],
            dst_ref=inbox.at[c],
            send_sem=send_sem.at[c],
            recv_sem=recv_sem.at[c],
            device_id={"seq": me + 1},
            device_id_type=MESH,
        )

    def place(owner, h):
        return pl.ds(pl.multiple_of(owner * width + h * HD, HD), HD)

    def rows_of(owner):
        return pl.ds(pl.multiple_of(owner * own_rows, CH), own_rows)

    def hand_over(h, k):
        to = lax.rem(mine + k, groups)
        return pltpu.make_async_remote_copy(
            src_ref=finished.at[h, rows_of(to), :],
            dst_ref=exchanged.at[:, place(mine, h)],
            send_sem=row_send.at[h, to],
            recv_sem=row_recv.at[h, mine],
            device_id={"head": to},
            device_id_type=MESH,
        )

    def take_over(h, k):
        source = lax.rem(mine + k, groups)
        return pltpu.make_async_remote_copy(
            src_ref=finished.at[h, rows_of(source), :],
            dst_ref=exchanged.at[:, place(source, h)],
            send_sem=row_send.at[h, source],
            recv_sem=row_recv.at[h, source],
            device_id={"head": source},
            device_id_type=MESH,
        )

    t = lax.broadcasted_iota(jnp.int32, (CH, CH), 0)
    s = lax.broadcasted_iota(jnp.int32, (CH, CH), 1)
    causal = t >= s
    twin = mine + 1 - 2 * lax.rem(mine, 2)
    depth = w_ref.shape[0]
    piece = depth // PARTS

    def weights(owner, part):
        return pl.ds(pl.multiple_of(owner * depth + part * piece, piece), piece)

    def share(k, part):
        to = twin if k == 0 else lax.rem(mine + 2 * k, groups)
        return pltpu.make_async_remote_copy(
            src_ref=w_ref.at[part * piece : (part + 1) * piece, :],
            dst_ref=gathered.at[weights(mine, part), :],
            send_sem=near_send.at[k, part],
            recv_sem=near_recv.at[k, part],
            device_id={"head": to},
            device_id_type=MESH,
        )

    def relay(k, part):
        source = lax.rem(mine + groups - 2 * k, groups)
        return pltpu.make_async_remote_copy(
            src_ref=gathered.at[weights(source, part), :],
            dst_ref=gathered.at[weights(source, part), :],
            send_sem=pass_send.at[k, part],
            recv_sem=pass_recv.at[k, part],
            device_id={"head": twin},
            device_id_type=MESH,
        )

    keep = pltpu.make_async_copy(w_ref, gathered.at[weights_of(mine, depth), :], own_sem)
    keep.start()
    for part in range(PARTS):
        for k in range(1, groups // 2):
            share(k, part).start()
    for part in range(PARTS):
        share(0, part).start()

    for h in range(local_heads):

        def pass_on(m, carry):
            c = h * M + m

            @pl.when(me > 0)
            def _():
                copy(c).wait_recv()

            arrived = inbox[c].astype(jnp.float32)
            current[m] = arrived

            @pl.when(me < size - 1)
            def _():
                outbox[c] = (prod_ref[c] * arrived + mem_ref[c]).astype(jnp.bfloat16)
                copy(c).start()

            return carry

        lax.fori_loop(0, M, pass_on, 0)
        cols = slice(h * HD, (h + 1) * HD)

        def block(b, carry):
            rows = pl.ds(pl.multiple_of(b * CH, CH), CH)
            at = (b * local_heads + h) * 2
            entering = (
                state_ref[b * local_heads + h].astype(jnp.float32)
                + entry_ref[at] * current[chosen[at]]
                + entry_ref[at + 1] * current[chosen[at + 1]]
            ).astype(jnp.bfloat16)
            query, keys, values = q_ref[rows, cols], key_ref[rows, cols], v_ref[rows, cols]
            column = column_ref[rows, h : h + 1]
            line = line_ref[b, h : h + 1, :]
            gaps = jnp.where(causal, column - line, 0.0)
            decays = jnp.where(causal, jnp.exp(gaps), 0.0)
            scores = lax.dot_general(
                query, keys, (((1,), (1,)), ((), ())), preferred_element_type=jnp.float32
            )
            weighted = (scores * decays).astype(jnp.bfloat16)
            within = jnp.dot(weighted, values, preferred_element_type=jnp.float32)
            carried = jnp.dot(query, entering, preferred_element_type=jnp.float32)
            total = jnp.exp(column) * carried + (shares[at] + shares[at + 1]) * within
            scale = lax.rsqrt(jnp.mean(total * total, axis=-1, keepdims=True) + 1e-06)
            finished[h, rows, :] = (total * scale * gain_ref[:, cols]).astype(jnp.bfloat16)
            return carry

        lax.fori_loop(0, blocks, block, 0, unroll=4)
        for k in range(1, groups):
            hand_over(h, k).start()
        exchanged[:, place(mine, h)] = finished[h, rows_of(mine), :]

    for part in range(PARTS):
        for k in range(1, groups // 2):
            share(k, part).wait_recv()
            relay(k, part).start()

    for h in range(local_heads):
        for k in range(1, groups):
            take_over(h, k).wait_recv()

    keep.wait()
    for part in range(PARTS):
        share(0, part).wait_recv()
        for k in range(1, groups // 2):
            relay(k, part).wait_recv()
            relay(k, part).wait_send()
        for k in range(groups // 2):
            share(k, part).wait_send()

    @pl.when(me < size - 1)
    def _():
        def drain(c, carry):
            copy(c).wait_send()
            return carry

        lax.fori_loop(0, pieces, drain, 0)

    for h in range(local_heads):
        for k in range(1, groups):
            hand_over(h, k).wait_send()


def per_device(
    tokens, w_query, w_key, w_value, w_out, norm_gain, forget_rate, routing, memory_blend_share
):
    tok_rows = tokens.shape[0]
    width = w_query.shape[1]
    local_heads = width // HD
    num_blocks = tok_rows // CH
    groups = lax.axis_size("head")
    own_rows = tok_rows // groups
    pieces = local_heads * M

    def project(weight):
        return jnp.dot(tokens, weight, preferred_element_type=jnp.float32).astype(jnp.bfloat16)

    key_raw, value_rows, query = project(w_key), project(w_value), project(w_query)
    chosen, shares = routing.reshape(-1), memory_blend_share.reshape(-1)
    smem = pl.BlockSpec(memory_space=SMEM)
    vmem = pl.BlockSpec(memory_space=VMEM)
    keys, states, memory, columns, lines, entry, products = pl.pallas_call(
        local_kernel,
        out_shape=(
            jax.ShapeDtypeStruct((tok_rows, width), jnp.bfloat16),
            jax.ShapeDtypeStruct((num_blocks * local_heads, HD, HD), jnp.bfloat16),
            jax.ShapeDtypeStruct((pieces, HD, HD), jnp.float32),
            jax.ShapeDtypeStruct((tok_rows, local_heads), jnp.float32),
            jax.ShapeDtypeStruct((num_blocks, local_heads, CH), jnp.float32),
            jax.ShapeDtypeStruct((num_blocks * local_heads * 2, 1, HD), jnp.float32),
            jax.ShapeDtypeStruct((pieces, 1, HD), jnp.float32),
        ),
        in_specs=[smem] * 2 + [vmem] * 3,
        out_specs=(vmem,) * 7,
        compiler_params=pltpu.CompilerParams(vmem_limit_bytes=LIMIT),
        name="local",
    )(chosen, shares, key_raw, value_rows, forget_rate)
    exchanged, whole_out = pl.pallas_call(
        chain_kernel,
        out_shape=(
            jax.ShapeDtypeStruct((own_rows, groups * width), jnp.bfloat16),
            jax.ShapeDtypeStruct((groups * w_out.shape[0], w_out.shape[1]), jnp.bfloat16),
        ),
        in_specs=[smem] * 2 + [vmem] * 11,
        out_specs=(vmem, pl.BlockSpec(memory_space=pltpu.HBM)),
        scratch_shapes=[
            VMEM((pieces, HD, HD), jnp.bfloat16),
            VMEM((pieces, HD, HD), jnp.bfloat16),
            VMEM((M, HD, HD), jnp.float32),
            VMEM((local_heads, tok_rows, HD), jnp.bfloat16),
            pltpu.SemaphoreType.DMA((pieces,)),
            pltpu.SemaphoreType.DMA((pieces,)),
            pltpu.SemaphoreType.DMA((local_heads, groups)),
            pltpu.SemaphoreType.DMA((local_heads, groups)),
            pltpu.SemaphoreType.DMA,
            pltpu.SemaphoreType.DMA((groups // 2, PARTS)),
            pltpu.SemaphoreType.DMA((groups // 2, PARTS)),
            pltpu.SemaphoreType.DMA((groups // 2, PARTS)),
            pltpu.SemaphoreType.DMA((groups // 2, PARTS)),
        ],
        compiler_params=pltpu.CompilerParams(
            collective_id=0, has_side_effects=True, vmem_limit_bytes=LIMIT
        ),
        name="chain",
    )(
        chosen,
        shares,
        entry,
        products,
        memory,
        query,
        keys,
        value_rows,
        columns,
        lines,
        states,
        norm_gain[None],
        w_out,
    )
    result = jnp.dot(exchanged, whole_out, preferred_element_type=jnp.float32)
    return result.astype(jnp.bfloat16)


def solution(mesh):
    placed = (
        P("seq", None),
        P(None, "head"),
        P(None, "head"),
        P(None, "head"),
        P("head", None),
        P("head"),
        P("seq", "head"),
        P("seq", "head", None),
        P("seq", "head", None),
    )
    return jax.shard_map(
        per_device, mesh=mesh, in_specs=placed, out_specs=P(("seq", "head"), None), check_vma=False
    )
```

profile of v0, /device:TPU:1, one launch (start us, length us, event | category | flops | bytes accessed | tf_op | source)
XLA Modules:
  0.0 102.2 jit_solution(12652827400129761560)
XLA Ops:
  0.0 0.0 copy-start
  0.0 0.9 copy.13
  0.9 0.7 reshape.6.chosen
  1.6 0.8 copy.14
  2.4 0.6 reshape.7.shares
  3.1 1.7 %copy.15.rate_ref = f32[1024,4]{1,0:T(8,128)} copy(f32[1024,4]{0,1:T(4,128)} %param.15) | data formatting | bytes 32768 | tf_op args[6]
  4.8 0.0 copy-done
  4.8 0.0 copy-start.1
  4.8 0.0 copy-start.2
  4.8 5.7 %convolution_convert_fusion.2.v_ref = bf16[1024,512]{1,0:T(8,128)(2,1)} fusion(bf16[1024,2048]{1,0:T(8,128)(2,1)} %param.9, bf16[2048,512]{1,0:T(8,128)(2,1)S(1)} %copy-done), kind=kOutput, calls=%fused_computation.2 | convolution fusion | flops 2148007936 | bytes 7340032 | tf_op jit(solution)/shard_map/dot_general | solution.py:323
  10.5 0.0 copy-done.1
  10.5 0.0 copy-done.2
  10.5 0.0 copy-start.3
  10.5 3.3 %convolution_convert_fusion.1.q_ref = bf16[1024,512]{1,0:T(8,128)(2,1)} fusion(bf16[1024,2048]{1,0:T(8,128)(2,1)S(1)} %copy-done.1, bf16[2048,512]{1,0:T(8,128)(2,1)S(1)} %copy-done.2), kind=kOutput, calls=%fused_computation.1 | convolution fusion | flops 2148007936 | bytes 7340032 | tf_op jit(solution)/shard_map/dot_general | solution.py:323
  13.8 0.0 copy-done.3
  13.8 3.3 %convolution_convert_fusion.3.k_ref = bf16[1024,512]{1,0:T(8,128)(2,1)} fusion(bf16[1024,2048]{1,0:T(8,128)(2,1)S(1)} %copy-done.1, bf16[2048,512]{1,0:T(8,128)(2,1)S(1)} %copy-done.3), kind=kOutput, calls=%fused_computation.3 | convolution fusion | flops 2148007936 | bytes 7340032 | tf_op jit(solution)/shard_map/dot_general | solution.py:323
  17.1 11.1 %local.1 = (bf16[1024,512]{1,0:T(8,128)(2,1)}, bf16[64,128,128]{2,1,0:T(8,128)(2,1)}, f32[32,128,128]{2,1,0:T(8,128)}, f32[1024,4]{1,0:T(8,128)}, f32[16,4,64]{2...) custom-call(s32[128]{0:T(128)} %reshape.6.chosen, f32[128]{0:T(128)} %reshape.7.shares, ...), custom_call_target="tpu_custom_call" | custom-call | tf_op jit(solution)/shard_map/local/pallas_call | solution.py:329
  28.3 66.9 %chain.1 = (bf16[256,2048]{1,0:T(8,128)(2,1)}, bf16[2048,2048]{1,0:T(8,128)(2,1)}) custom-call(s32[128]{0:T(128)} %reshape.6.chosen, f32[128]{0:T(128)} %reshape.7.shares, f32[128,1,128]{2,1,0:T(1,128)} %get-tuple-element.14.entry_ref, f32[32,1,128]{2,1,0:T(1,128)} %get-tuple-element.15.prod_ref, f32[32,128,128]{2,1,0:T(8,128)} %get-tuple-element.16.mem_ref, ...), custom_call_target="tpu_custom_call" | custom-call | tf_op jit(solution)/shard_map/chain/pallas_call | solution.py:345
  95.2 7.0 %convolution_convert_fusion = bf16[256,2048]{1,0:T(8,128)(2,1)} fusion(bf16[256,2048]{1,0:T(8,128)(2,1)} %get-tuple-element.21, bf16[2048,2048]{1,0:T(8,128)(2,1)} %get-tuple-element.22), kind=kOutput, calls=%fused_computation | convolution fusion | flops 2148007936 | bytes 10485760 | tf_op jit(solution)/shard_map/dot_general | solution.py:387
Async XLA Ops:
  0.0 4.8 %copy-start = (bf16[2048,512]{1,0:T(8,128)(2,1)S(1)}, bf16[2048,512]{1,0:T(8,128)(2,1)}, u32[]{:S(2)}) copy-start(bf16[2048,512]{1,0:T(8,128)(2,1)} %param.12) | copy-start | bytes 6291460
  4.8 5.7 %copy-start.1 = (bf16[1024,2048]{1,0:T(8,128)(2,1)S(1)}, bf16[1024,2048]{1,0:T(8,128)(2,1)}, u32[]{:S(2)}) copy-start(bf16[1024,2048]{1,0:T(8,128)(2,1)} %param.9) | copy-start | bytes 12582916
  4.8 5.7 %copy-start.2 = (bf16[2048,512]{1,0:T(8,128)(2,1)S(1)}, bf16[2048,512]{1,0:T(8,128)(2,1)}, u32[]{:S(2)}) copy-start(bf16[2048,512]{1,0:T(8,128)(2,1)} %param.10) | copy-start | bytes 6291460
  10.5 3.3 %copy-start.3 = (bf16[2048,512]{1,0:T(8,128)(2,1)S(1)}, bf16[2048,512]{1,0:T(8,128)(2,1)}, u32[]{:S(2)}) copy-start(bf16[2048,512]{1,0:T(8,128)(2,1)} %param.11) | copy-start | bytes 6291460
where the time goes:
time: 103 us; the launch traced here: 102 us
  Pallas kernels  78.1 us (76%)
  matrix products  19.4 us (19%)
  local copies, waits for them, and re-layouts  4.79 us (5%)
    pallas_call x1, Pallas kernels, per_device(): pl.pallas_call(chain_kernel, out_shape=(jax.ShapeDtypeStruct((own_rows, g...  66.9 us
    dot_general x3, matrix products, project(): jnp.dot(tokens, weight, preferred_element_type=jnp.float32)  12.3 us
    pallas_call x1, Pallas kernels, per_device(): pl.pallas_call(local_kernel, out_shape=(jax.ShapeDtypeStruct((tok_rows, w...  11.1 us
    dot_general x1, matrix products, per_device(): result = jnp.dot(exchanged, whole_out, preferred_element_type=jnp.float32)  7.02 us
    unnamed x11, local copies, waits for them, and re-layouts  3.47 us

commit v1 on v0

v1 whole, which is shorter than its diff:
```python
import jax
import jax.numpy as jnp
from jax import lax
from jax.experimental import pallas as pl
from jax.experimental.pallas import tpu as pltpu
from jax.sharding import PartitionSpec as P

HD = 128
M = 8
CH = 64
TILE = 256
SUB = 2
WAIT_SLOTS = 4
HOP_SLOTS = 3

HIGHEST = lax.Precision.HIGHEST
MESH = pl.DeviceIdType.MESH
VMEM = pltpu.VMEM
DMA = pltpu.SemaphoreType.DMA
LIMIT = 64 * 1024 * 1024 - 128 * 1024
BF = jnp.bfloat16
F32 = jnp.float32


def aligned(start, step):
    return pl.multiple_of(start, step)


def dot(a, b, **kw):
    return jnp.dot(a, b, preferred_element_type=F32, **kw)


def layer_kernel(
    rates,
    routing,
    shares,
    gain,
    tokens,
    w_query,
    w_key,
    w_value,
    w_out,
    out,
    tok,
    wkv,
    wq,
    q,
    kt,
    ktf,
    v,
    ks,
    memb,
    p1in,
    zin,
    zout,
    yout,
    sin,
    rowbuf,
    cum,
    tail,
    endr,
    ei_ref,
    e_ref,
    sh_ref,
    wrow,
    prod,
    prodpar,
    coef,
    cr,
    cb,
    qs,
    intra,
    fin,
    exch,
    wfull,
    oacc,
    tok_sem,
    wkv_sem,
    wq_sem,
    own_sem,
    prod_sem,
    p1_sem,
    z_sem,
    y_sem,
    row_sem,
    twin_sem,
    x_sem,
    xt_sem,
    zw_sem,
    zt_sem,
):
    size, me = lax.axis_size("seq"), lax.axis_index("seq")
    groups, mine = lax.axis_size("head"), lax.axis_index("head")
    heads, rows_all = rates.shape
    depth = tokens.shape[1]
    blocks = rows_all // CH
    tiles = rows_all // TILE
    per_tile = TILE // CH
    own_rows = rows_all // groups
    planes = size // 2
    chips = groups // 2
    parity = lax.rem(me, 2)
    plane = lax.div(me, 2)
    even = lax.rem(plane, 2)
    partner = me + 1 - 2 * parity
    zmate = me + 2 - 4 * even
    twin = mine + 1 - 2 * lax.rem(mine, 2)
    units = heads * SUB
    column_rows = M * HD // 2
    unit_rows = column_rows // SUB
    half = HD // 2
    barrier = pltpu.get_barrier_semaphore()

    def tok_copy(i):
        rows = pl.ds(aligned(i * TILE, TILE), TILE)
        return pltpu.make_async_copy(tokens.at[rows, :], tok.at[rows, :], tok_sem.at[i])

    def wkv_copy(h, side):
        cols = pl.ds(aligned(h * HD, HD), HD)
        source = w_value if side else w_key
        return pltpu.make_async_copy(
            source.at[:, cols],
            wkv.at[h, :, side * HD : (side + 1) * HD],
            wkv_sem.at[h, side],
        )

    def wq_copy(i):
        cols = pl.ds(aligned(i * 2 * HD, 2 * HD), 2 * HD)
        return pltpu.make_async_copy(w_query.at[:, cols], wq.at[i], wq_sem.at[i])

    def block_of(owner):
        return pl.ds(aligned(owner * HD, HD), HD)

    def half_of(owner, side):
        return pl.ds(aligned(owner * HD + side * half, half), half)

    own_copy = pltpu.make_async_copy(w_out, wfull.at[:, block_of(mine), :], own_sem)

    def seq_copy(src, dst, send, recv, to):
        return pltpu.make_async_remote_copy(
            src_ref=src,
            dst_ref=dst,
            send_sem=send,
            recv_sem=recv,
            device_id={"seq": to},
            device_id_type=MESH,
        )

    def head_copy(src, dst, send, recv, to):
        return pltpu.make_async_remote_copy(
            src_ref=src,
            dst_ref=dst,
            send_sem=send,
            recv_sem=recv,
            device_id={"head": to},
            device_id_type=MESH,
        )

    prod_copy = seq_copy(prod, prodpar, prod_sem.at[0], prod_sem.at[1], partner)

    def twin_copy(owner):
        return head_copy(
            w_out, wfull.at[:, block_of(owner), :], twin_sem.at[0], twin_sem.at[1], twin
        )

    def x_send(k, h):
        to = lax.rem(mine + 2 * k, groups)
        return head_copy(
            w_out.at[h, pl.ds(aligned(even * half, half), half), :],
            wfull.at[h, half_of(mine, even), :],
            x_sem.at[0, k, h],
            x_sem.at[1, k, h],
            to,
        )

    def x_recv(k, h):
        source = lax.rem(mine + groups - 2 * k, groups)
        place = wfull.at[h, half_of(source, even), :]
        return head_copy(place, place, x_sem.at[0, k, h], x_sem.at[1, k, h], source)

    def xt_copy(k, h, base):
        source = lax.rem(base + groups - 2 * k, groups)
        place = wfull.at[h, half_of(source, even), :]
        return head_copy(place, place, xt_sem.at[0, k, h], xt_sem.at[1, k, h], twin)

    def zw_copy(k, h, side):
        source = lax.rem(mine + groups - 2 * k, groups)
        place = wfull.at[h, half_of(source, side), :]
        return seq_copy(place, place, zw_sem.at[0, k, h], zw_sem.at[1, k, h], zmate)

    def zt_copy(k, h, base):
        source = lax.rem(base + groups - 2 * k, groups)
        place = wfull.at[h, half_of(source, 1 - even), :]
        return head_copy(place, place, zt_sem.at[0, k, h], zt_sem.at[1, k, h], twin)

    def p1_copy(u):
        h, sub = lax.div(u, SUB), lax.rem(u, SUB)
        rows = pl.ds(aligned((1 - parity) * column_rows + sub * unit_rows, unit_rows), unit_rows)
        return seq_copy(
            memb.at[h, rows, :], p1in.at[u], p1_sem.at[0, u], p1_sem.at[1, u], partner
        )

    def z_copy(u):
        return seq_copy(zout.at[u], zin.at[u], z_sem.at[0, u], z_sem.at[1, u], me + 2)

    def y_copy(u, side):
        h, sub = lax.div(u, SUB), lax.rem(u, SUB)
        rows = pl.ds(aligned(side * column_rows + sub * unit_rows, unit_rows), unit_rows)
        return seq_copy(yout.at[u], sin.at[h, rows, :], y_sem.at[0, u], y_sem.at[1, u], partner)

    def rows_of(owner):
        return pl.ds(aligned(owner * own_rows, own_rows), own_rows)

    def row_send(h, k):
        to = lax.rem(mine + k, groups)
        return head_copy(
            fin.at[h, rows_of(to), :],
            exch.at[h, :, block_of(mine)],
            row_sem.at[0, h, to],
            row_sem.at[1, h, mine],
            to,
        )

    def row_recv(h, k):
        source = lax.rem(mine + k, groups)
        return head_copy(
            fin.at[h, rows_of(source), :],
            exch.at[h, :, block_of(source)],
            row_sem.at[0, h, source],
            row_sem.at[1, h, source],
            source,
        )

    def loop(n, body):
        def step(i, carry):
            body(i)
            return carry

        lax.fori_loop(0, n, step, 0)

    for side in range(2):
        wkv_copy(0, side).start()
    for i in range(tiles):
        tok_copy(i).start()
    for h in range(1, heads):
        for side in range(2):
            wkv_copy(h, side).start()
    for i in range(heads // 2):
        wq_copy(i).start()

    pl.semaphore_signal(barrier, 1, device_id={"seq": partner}, device_id_type=MESH)

    @pl.when(plane > 0)
    def _():
        pl.semaphore_signal(barrier, 1, device_id={"seq": me - 2}, device_id_type=MESH)

    @pl.when(plane < planes - 1)
    def _():
        pl.semaphore_signal(barrier, 1, device_id={"seq": me + 2}, device_id_type=MESH)

    for k in range(1, groups):
        pl.semaphore_signal(
            barrier, 1, device_id={"head": lax.rem(mine + k, groups)}, device_id_type=MESH
        )

    lane = lax.broadcasted_iota(jnp.int32, (heads, rows_all), 1)
    spot = lax.rem(lane, CH)
    rate = rates[...]
    total = -rate
    later = -rate
    step = 1
    while step < CH:
        total = total + jnp.where(spot >= step, pltpu.roll(total, step, 1), 0.0)
        later = later + jnp.where(
            spot < CH - step, pltpu.roll(later, rows_all - step, 1), 0.0
        )
        step *= 2
    later = later + rate
    rowbuf[...] = jnp.zeros_like(rowbuf)
    rowbuf[0:heads, :] = total
    for h in range(heads):
        cum[h] = total[h : h + 1]
        tail[h] = jnp.exp(later[h : h + 1])
        endr[h] = (total + later)[h : h + 1]
    columns = jnp.transpose(rowbuf[...])
    for h in range(heads):
        cb[h] = jnp.broadcast_to(columns[:, h : h + 1], (rows_all, HD))

    spread = jnp.where(
        lax.div(lax.broadcasted_iota(jnp.int32, (blocks, rows_all), 1), CH)
        == lax.broadcasted_iota(jnp.int32, (blocks, rows_all), 0),
        1.0,
        0.0,
    )
    wide_lane = lax.broadcasted_iota(jnp.int32, (M, rows_all), 1)
    memory_id = lax.broadcasted_iota(jnp.int32, (M, rows_all), 0).astype(F32)

    for h in range(heads):
        named = dot(routing[h].astype(F32), spread)
        share = dot(shares[h], spread, precision=HIGHEST)
        first = named[0:1] == memory_id
        second = named[1:2] == memory_id
        written = jnp.where(first, 1.0, jnp.where(second, 1.0, 0.0))
        mix = jnp.where(first, share[0:1], jnp.where(second, share[1:2], 0.0))
        own = written * endr[h]
        upto = own
        step = CH
        while step < rows_all:
            upto = upto + jnp.where(wide_lane >= step, pltpu.roll(upto, step, 1), 0.0)
            step *= 2
        whole = upto[:, rows_all - 1 : rows_all]
        ei_ref[h] = upto
        e_ref[h] = upto - own
        sh_ref[h] = mix
        wrow[h] = written * jnp.exp(whole - upto) * tail[h]
        prod[h] = jnp.broadcast_to(jnp.exp(whole), (M, HD))

    waits = 1 + (groups - 1) + jnp.where(plane > 0, 1, 0) + jnp.where(plane < planes - 1, 1, 0)
    pl.semaphore_wait(barrier, waits)
    prod_copy.start()
    for h in range(heads):
        for k in range(1, chips):
            x_send(k, h).start()
    twin_copy(mine).start()
    own_copy.start()

    @pl.when(plane == 0)
    def _():
        zin[...] = jnp.zeros_like(zin)

    def chain_step(u):
        h, sub = lax.div(u, SUB), lax.rem(u, SUB)
        p1_copy(u).wait_recv()

        @pl.when(plane > 0)
        def _():
            z_copy(u).wait_recv()

        start = aligned(parity * column_rows + sub * unit_rows, unit_rows)
        for i in range(unit_rows // HD):
            part = pl.ds(i * HD, HD)
            rows = pl.ds(aligned(start + i * HD, HD), HD)
            m = parity * (M // 2) + sub * (unit_rows // HD) + i
            arrived = zin[u, part, :].astype(F32)
            mine_mem = memb[h, rows, :].astype(F32)
            other_mem = p1in[u, part, :].astype(F32)
            mine_prod = prod[h, pl.ds(m, 1), :]
            other_prod = prodpar[h, pl.ds(m, 1), :]
            lead = parity == 0
            early_mem = jnp.where(lead, mine_mem, other_mem)
            late_mem = jnp.where(lead, other_mem, mine_mem)
            early_prod = jnp.where(lead, mine_prod, other_prod)
            late_prod = jnp.where(lead, other_prod, mine_prod)
            stepped = early_prod * arrived + early_mem
            zout[u, part, :] = (late_prod * stepped + late_mem).astype(BF)
            yout[u, part, :] = jnp.where(lead, stepped, arrived).astype(BF)
            sin[h, rows, :] = jnp.where(lead, arrived, stepped).astype(BF)

        @pl.when(plane < planes - 1)
        def _():
            z_copy(u).start()

        y_copy(u, parity).start()

    def chain_slot(slot):
        u = slot - WAIT_SLOTS - HOP_SLOTS * plane

        @pl.when(jnp.logical_and(u >= 0, u < units))
        def _():
            chain_step(u)

    def service(j):
        if isinstance(j, int) and j >= heads:
            pass
        else:
            for k in range(1, chips):
                x_recv(k, j).wait_recv()
                zw_copy(k, j, even).start()
                xt_copy(k, j, mine).start()
        if j > 0:
            for k in range(1, chips):
                zw_copy(k, j - 1, 1 - even).wait_recv()
                zt_copy(k, j - 1, mine).start()

    def first_stage(h):
        for side in range(2):
            wkv_copy(h, side).wait()

        def project(i):
            @pl.when(h == 0)
            def _():
                tok_copy(i).wait()

            rows = pl.ds(aligned(i * TILE, TILE), TILE)
            both = dot(tok[rows, :], wkv[h])
            v[h, rows, :] = both[:, HD:].astype(BF)
            wide = both[:, :HD].astype(BF).astype(F32)
            keys = wide * lax.rsqrt(jnp.sum(wide * wide, axis=-1, keepdims=True) + 1e-06)
            turned = jnp.transpose(keys.astype(BF).astype(F32))
            ktf[:, rows] = turned
            kt[h, :, rows] = turned.astype(BF)

        loop(tiles, project)
        chain_slot(2 * h)

        @pl.when(h == heads // 2)
        def _():
            service(0)

        @pl.when(h == 0)
        def _():
            prod_copy.wait_recv()

        for m in range(M):
            ks[m * HD : (m + 1) * HD, :] = (ktf[...] * wrow[h, m : m + 1, :]).astype(BF)

        def state(i):
            rows = pl.ds(aligned(i * column_rows, column_rows), column_rows)
            memb[h, rows, :] = dot(ks[rows, :], v[h]).astype(BF)

        loop(2, state)
        for sub in range(SUB):
            p1_copy(h * SUB + sub).start()
        chain_slot(2 * h + 1)

    loop(heads, first_stage)
    slot = 2 * heads
    service(1)

    def query_stage(i):
        wq_copy(i).wait()
        for part in range(2):
            n = rows_all // 2
            rows = slice(part * n, (part + 1) * n)
            both = dot(tok[rows, :], wq[i]).astype(BF)
            q[2 * i, rows, :] = both[:, :HD]
            q[2 * i + 1, rows, :] = both[:, HD:]
            chain_slot(slot + 2 * i + part)

    loop(heads // 2, query_stage)
    slot += heads

    tile_lane = lax.broadcasted_iota(jnp.int32, (CH, TILE), 1)
    tile_row = lax.broadcasted_iota(jnp.int32, (CH, TILE), 0)

    def second_stage(h):
        upto, before, mix, decay = ei_ref[h], e_ref[h], sh_ref[h], tail[h]
        written = jnp.where(mix > 0.0, 1.0, 0.0)
        amount = jnp.sum(mix, axis=0, keepdims=True)
        reads = mix * jnp.exp(before)
        for b in range(blocks):
            at = slice(b * CH, b * CH + 1)
            n = (b // per_tile + 1) * TILE
            coef[h, b] = jnp.broadcast_to(reads[:, at], (M, HD))
            gap = jnp.minimum(before[:, at] - upto[:, :n], 0.0)
            pull = jnp.sum(mix[:, at] * written[:, :n] * jnp.exp(gap), axis=0, keepdims=True)
            position = lax.broadcasted_iota(jnp.int32, (1, n), 1)
            cr[h, b : b + 1, :n] = jnp.where(
                position < b * CH,
                pull * decay[:, :n],
                jnp.where(position < (b + 1) * CH, amount[:, :n], 0.0),
            )

        @pl.when(lax.rem(h, 2) == 1)
        def _():
            j = lax.div(h, 2) + 2

            @pl.when(j < heads)
            def _():
                service_at(j)

        for g in range(tiles):
            rows = slice(g * TILE, (g + 1) * TILE)
            query = q[h, rows, :]
            growth = jnp.exp(cb[h, rows, :])
            acc = jnp.zeros((TILE, HD), F32)
            for t in range(g):
                cols = slice(t * TILE, (t + 1) * TILE)
                scores = dot(query, kt[h, :, cols])
                parts = [
                    (
                        scores[i * CH : (i + 1) * CH]
                        * cr[h, g * per_tile + i : g * per_tile + i + 1, cols]
                    ).astype(BF)
                    for i in range(per_tile)
                ]
                acc = acc + dot(jnp.concatenate(parts, axis=0), v[h, cols, :])
            scores = dot(query, kt[h, :, rows])
            parts = []
            for i in range(per_tile):
                b = g * per_tile + i
                own = cb[h, b * CH : (b + 1) * CH, :]
                col = jnp.concatenate([own] * (TILE // HD), axis=1)
                inside = lax.div(tile_lane, CH) == i
                gap = col - jnp.where(inside, cum[h, :, rows], 0.0)
                factor = jnp.exp(jnp.minimum(gap, 0.0)) * cr[h, b : b + 1, rows]
                factor = jnp.where(tile_lane <= tile_row + i * CH, factor, 0.0)
                parts.append((scores[i * CH : (i + 1) * CH] * factor).astype(BF))
            near = dot(jnp.concatenate(parts, axis=0), v[h, rows, :])
            intra[h, rows, :] = acc * growth + near
            grown = query.astype(F32) * growth
            for i in range(per_tile):
                b = g * per_tile + i
                piece = grown[i * CH : (i + 1) * CH]
                for m in range(M):
                    qs[h, b * CH : (b + 1) * CH, m * HD : (m + 1) * HD] = (
                        piece * coef[h, b, m : m + 1, :]
                    ).astype(BF)
            if g % 2 == 1:
                chain_slot(slot + h * (tiles // 2) + g // 2)

    def service_at(j):
        for k in range(1, chips):
            x_recv(k, j).wait_recv()
            zw_copy(k, j, even).start()
            xt_copy(k, j, mine).start()
            zw_copy(k, j - 1, 1 - even).wait_recv()
            zt_copy(k, j - 1, mine).start()

    loop(heads, second_stage)
    slot += heads * (tiles // 2)
    last_slot = WAIT_SLOTS + HOP_SLOTS * (planes - 1) + units
    if last_slot > slot:
        loop(last_slot - slot, lambda i: chain_slot(slot + i))

    def finish(h):
        for sub in range(SUB):
            y_copy(h * SUB + sub, 1 - parity).wait_recv()

        def piece(k):
            owner = lax.rem(mine + k + 1, groups)
            rows = rows_of(owner)
            whole = intra[h, rows, :] + dot(qs[h, rows, :], sin[h])
            scale = lax.rsqrt(jnp.mean(whole * whole, axis=-1, keepdims=True) + 1e-06)
            fin[h, rows, :] = (whole * scale * gain[h]).astype(BF)

            @pl.when(k < groups - 1)
            def _():
                row_send(h, k + 1).start()

        loop(groups, piece)
        exch[h, :, block_of(mine)] = fin[h, rows_of(mine), :]

    def emit(h, opening, closing):
        for k in range(1, groups):
            row_recv(h, k).wait_recv()
        for k in range(1, chips):
            xt_copy(k, h, twin).wait_recv()
            zt_copy(k, h, twin).wait_recv()
        for part in range(depth // 512):
            cols = slice(part * 512, (part + 1) * 512)
            more = dot(exch[h], wfull[h, :, cols])
            if not opening:
                more = oacc[:, cols] + more
            if closing:
                out[:, cols] = more.astype(BF)
            else:
                oacc[:, cols] = more

    for h in range(heads):
        finish(h)
        if h == 0:
            for k in range(1, chips):
                zw_copy(k, heads - 1, 1 - even).wait_recv()
                zt_copy(k, heads - 1, mine).start()
        if h == 1:
            own_copy.wait()
            twin_copy(twin).wait_recv()
        if h > 0:
            emit(h - 1, h == 1, False)
    emit(heads - 1, heads == 1, True)

    prod_copy.wait_send()
    twin_copy(mine).wait_send()

    def drain_weights(h):
        for k in range(1, chips):
            x_send(k, h).wait_send()
            xt_copy(k, h, mine).wait_send()
            zw_copy(k, h, even).wait_send()
            zt_copy(k, h, mine).wait_send()
        for k in range(1, groups):
            row_send(h, k).wait_send()

    loop(heads, drain_weights)

    def drain_units(u):
        p1_copy(u).wait_send()
        y_copy(u, parity).wait_send()

        @pl.when(plane < planes - 1)
        def _():
            z_copy(u).wait_send()

    loop(units, drain_units)


def per_device(
    tokens, w_query, w_key, w_value, w_out, norm_gain, forget_rate, routing, memory_blend_share
):
    rows, depth = tokens.shape
    width = w_query.shape[1]
    heads = width // HD
    blocks = rows // CH
    groups, size = lax.axis_size("head"), lax.axis_size("seq")
    assert size % 4 == 0 and groups % 2 == 0 and heads % 2 == 0 and rows % TILE == 0
    chips = groups // 2
    own_rows = rows // groups
    units = heads * SUB
    unit_rows = M * HD // 2 // SUB
    vmem = pl.BlockSpec(memory_space=VMEM)
    hbm = pl.BlockSpec(memory_space=pl.ANY)
    return pl.pallas_call(
        layer_kernel,
        out_shape=jax.ShapeDtypeStruct((own_rows, depth), BF),
        in_specs=[vmem] * 4 + [hbm] * 5,
        out_specs=vmem,
        scratch_shapes=[
            VMEM((rows, depth), BF),
            VMEM((heads, depth, 2 * HD), BF),
            VMEM((heads // 2, depth, 2 * HD), BF),
            VMEM((heads, rows, HD), BF),
            VMEM((heads, HD, rows), BF),
            VMEM((HD, rows), F32),
            VMEM((heads, rows, HD), BF),
            VMEM((M * HD, rows), BF),
            VMEM((heads, M * HD, HD), BF),
            VMEM((units, unit_rows, HD), BF),
            VMEM((units, unit_rows, HD), BF),
            VMEM((units, unit_rows, HD), BF),
            VMEM((units, unit_rows, HD), BF),
            VMEM((heads, M * HD, HD), BF),
            VMEM((8, rows), F32),
            VMEM((heads, 1, rows), F32),
            VMEM((heads, 1, rows), F32),
            VMEM((heads, 1, rows), F32),
            VMEM((heads, M, rows), F32),
            VMEM((heads, M, rows), F32),
            VMEM((heads, M, rows), F32),
            VMEM((heads, M, rows), F32),
            VMEM((heads, M, HD), F32),
            VMEM((heads, M, HD), F32),
            VMEM((heads, blocks, M, HD), F32),
            VMEM((heads, blocks, rows), F32),
            VMEM((heads, rows, HD), F32),
            VMEM((heads, rows, M * HD), BF),
            VMEM((heads, rows, HD), F32),
            VMEM((heads, rows, HD), BF),
            VMEM((heads, own_rows, groups * HD), BF),
            VMEM((heads, groups * HD, depth), BF),
            VMEM((own_rows, depth), F32),
            DMA((rows // TILE,)),
            DMA((heads, 2)),
            DMA((heads // 2,)),
            DMA,
            DMA((2,)),
            DMA((2, units)),
            DMA((2, units)),
            DMA((2, units)),
            DMA((2, heads, groups)),
            DMA((2,)),
            DMA((2, chips, heads)),
            DMA((2, chips, heads)),
            DMA((2, chips, heads)),
            DMA((2, chips, heads)),
        ],
        compiler_params=pltpu.CompilerParams(
            collective_id=0, has_side_effects=True, vmem_limit_bytes=LIMIT
        ),
        name="layer",
    )(
        forget_rate.T,
        jnp.transpose(routing, (1, 2, 0)),
        jnp.transpose(memory_blend_share, (1, 2, 0)),
        norm_gain.reshape(heads, 1, HD),
        tokens,
        w_query,
        w_key,
        w_value,
        w_out.reshape(heads, HD, depth),
    )


def solution(mesh):
    placed = (
        P("seq", None),
        P(None, "head"),
        P(None, "head"),
        P(None, "head"),
        P("head", None),
        P("head"),
        P("seq", "head"),
        P("seq", "head", None),
        P("seq", "head", None),
    )
    return jax.shard_map(
        per_device, mesh=mesh, in_specs=placed, out_specs=P(("seq", "head"), None), check_vma=False
    )
```

time: 103 us -> 65.8 us (0.64)
  matrix products: 19.4 us -> 0 us
  Pallas kernels: 78.1 us -> 63.3 us
  local copies, waits for them, and re-layouts: 4.79 us -> 2.3 us
    dot_general x4 -> x0, matrix products: 19.4 us -> none  [the longest x3 12.3 us: project(): jnp.dot(tokens, weight, preferred_element_type=jnp.float32)]
    pallas_call x2 -> x1, Pallas kernels: 78.1 us -> 63.3 us  [per_device(): pl.pallas_call(layer_kernel, out_shape=jax.ShapeDtypeStruct((own_rows, de...]
    reshape x2 -> x0, local copies, waits for them, and re-layouts: 1.33 us -> none  [per_device(): chosen, shares = (routing.reshape(-1), memory_blend_share.reshape(-1))]
    unnamed x11 -> x1, local copies, waits for them, and re-layouts: 3.47 us -> 2.3 us
where the time goes in v1:
time: 65.8 us; the launch traced here: 65.6 us
  Pallas kernels  63.3 us (96%)
  local copies, waits for them, and re-layouts  2.3 us (3%)
    pallas_call x1, Pallas kernels, per_device(): pl.pallas_call(layer_kernel, out_shape=jax.ShapeDtypeStruct((own_rows, de...  63.3 us
    unnamed x1, local copies, waits for them, and re-layouts  2.3 us

profile of v1, /device:TPU:1, one launch (start us, length us, event | category | flops | bytes accessed | tf_op | source)
XLA Modules:
  0.0 65.6 jit_solution(4162356067440862951)
XLA Ops:
  0.0 63.3 %layer.1 = bf16[256,2048]{1,0:T(8,128)(2,1)} custom-call(f32[4,1024]{1,0:T(4,128)} %bitcast.6, s32[4,2,16]{2,1,0:T(2,128)} %bitcast.7, f32[4,2,16]{2,1,0:T(2,128)} %bitcast.8, f32[4,1,128]{2,1,0:T(1,128)} %bitcast.9, bf16[1024,2048]{1,0:T(8,128)(2,1)} %tokens.1, bf16[2048,512]{1,0:T(8,128)(2,1)} %w_query.1, bf16[2048,512]{1,0:T(8,128)(2,1)} %w_key.1, ...), custom_call_target="tpu_custom_call" | custom-call | tf_op jit(solution)/shard_map/layer/pallas_call | solution.py:613
  63.3 2.3 %copy.11 = bf16[256,2048]{1,0:T(8,128)(2,1)} copy(bf16[256,2048]{1,0:T(8,128)(2,1)} %layer.1) | data formatting | bytes 2097152

commit v2 on v1

v2 whole, which is shorter than its diff:
```python
import jax
import jax.numpy as jnp
from jax import lax
from jax.experimental import pallas as pl
from jax.experimental.pallas import tpu as pltpu
from jax.sharding import PartitionSpec as P

HD = 128
M = 8
CH = 64
TILE = 256
SUB = 2
WAIT_TICKS = 4
HOP_TICKS = 2
PARTS = 2
PIECES = 2

HIGHEST = lax.Precision.HIGHEST
MESH = pl.DeviceIdType.MESH
VMEM = pltpu.VMEM
DMA = pltpu.SemaphoreType.DMA
LIMIT = 64 * 1024 * 1024 - 128 * 1024
BF = jnp.bfloat16
F32 = jnp.float32


def aligned(start, step):
    return pl.multiple_of(start, step)


def dot(a, b, **kw):
    return jnp.dot(a, b, preferred_element_type=F32, **kw)


def layer_kernel(
    rates,
    routing,
    shares,
    gain,
    tokens,
    w_query,
    w_key,
    w_value,
    w_out,
    out,
    tok,
    wkv,
    wq,
    both,
    q,
    kt,
    v,
    ks,
    memb,
    p1in,
    zin,
    zout,
    yout,
    sin,
    rowbuf,
    cum,
    tail,
    endr,
    ei_ref,
    e_ref,
    sh_ref,
    wrow,
    prod,
    prodpar,
    coef,
    cr,
    cb,
    qs,
    intra,
    fin,
    exch,
    wfull,
    oacc,
    tok_sem,
    wkv_sem,
    wq_sem,
    own_sem,
    prod_sem,
    p1_sem,
    z_sem,
    y_sem,
    row_sem,
    twin_sem,
    x_sem,
    xt_sem,
    zw_sem,
    up_sem,
    zt_sem,
):
    size, me = lax.axis_size("seq"), lax.axis_index("seq")
    groups, mine = lax.axis_size("head"), lax.axis_index("head")
    heads, rows_all = rates.shape
    depth = tokens.shape[1]
    blocks = rows_all // CH
    tiles = rows_all // TILE
    per_tile = TILE // CH
    own_rows = rows_all // groups
    planes = size // 2
    chips = groups // 2
    chip, core = lax.div(mine, 2), lax.rem(mine, 2)
    parity = lax.rem(me, 2)
    plane = lax.div(me, 2)
    even = lax.rem(plane, 2)
    partner = me + 1 - 2 * parity
    twin = mine + 1 - 2 * core
    units = heads * SUB
    column_rows = M * HD // 2
    unit_rows = column_rows // SUB
    half = HD // 2
    part_rows = half // PARTS
    piece_rows = part_rows // PIECES
    parts = heads * PARTS
    barrier = pltpu.get_barrier_semaphore()

    def tok_copy(i):
        rows = pl.ds(aligned(i * TILE, TILE), TILE)
        return pltpu.make_async_copy(tokens.at[rows, :], tok.at[rows, :], tok_sem.at[i])

    def wkv_copy(h, side):
        source = w_value if side else w_key
        return pltpu.make_async_copy(
            source.at[:, h * HD : (h + 1) * HD],
            wkv.at[h, :, side * HD : (side + 1) * HD],
            wkv_sem.at[h, side],
        )

    def wq_copy(i):
        return pltpu.make_async_copy(
            w_query.at[:, i * 2 * HD : (i + 1) * 2 * HD], wq.at[i], wq_sem.at[i]
        )

    def block_of(owner):
        return pl.ds(aligned(owner * HD, HD), HD)

    def place(owner, side, part):
        start = owner * HD + side * half + part * part_rows
        return pl.ds(aligned(start, part_rows), part_rows)

    def small_place(owner, side, part, piece):
        start = owner * HD + side * half + part * part_rows + piece * piece_rows
        return pl.ds(aligned(start, piece_rows), piece_rows)

    own_copy = pltpu.make_async_copy(w_out, wfull.at[:, block_of(mine), :], own_sem)

    def seq_copy(src, dst, send, recv, to):
        return pltpu.make_async_remote_copy(
            src_ref=src,
            dst_ref=dst,
            send_sem=send,
            recv_sem=recv,
            device_id={"seq": to},
            device_id_type=MESH,
        )

    def head_copy(src, dst, send, recv, to):
        return pltpu.make_async_remote_copy(
            src_ref=src,
            dst_ref=dst,
            send_sem=send,
            recv_sem=recv,
            device_id={"head": to},
            device_id_type=MESH,
        )

    def prod_copy(h):
        return seq_copy(
            prod.at[h], prodpar.at[h], prod_sem.at[0, h], prod_sem.at[1, h], partner
        )

    def twin_copy(owner):
        return head_copy(
            w_out, wfull.at[:, block_of(owner), :], twin_sem.at[0], twin_sem.at[1], twin
        )

    def behind(base, k):
        return lax.rem(base + groups - 2 * k, groups)

    def x_send(k, j):
        h, part = j // PARTS, j % PARTS
        to = lax.rem(mine + 2 * k, groups)
        start = aligned(even * half + part * part_rows, part_rows)
        return head_copy(
            w_out.at[h, pl.ds(start, part_rows), :],
            wfull.at[h, place(mine, even, part), :],
            x_sem.at[0, k, j],
            x_sem.at[1, k, j],
            to,
        )

    def x_recv(k, j):
        spot = wfull.at[j // PARTS, place(behind(mine, k), even, j % PARTS), :]
        return head_copy(spot, spot, x_sem.at[0, k, j], x_sem.at[1, k, j], behind(mine, k))

    def xt_copy(k, j, base):
        spot = wfull.at[j // PARTS, place(behind(base, k), even, j % PARTS), :]
        return head_copy(spot, spot, xt_sem.at[0, k, j], xt_sem.at[1, k, j], twin)

    def zw_copy(k, j, piece, side, sems, to):
        spot = wfull.at[j // PARTS, small_place(behind(mine, k), side, j % PARTS, piece), :]
        return seq_copy(
            spot, spot, sems.at[k, j, piece], zw_sem.at[1, k, j, piece], to
        )

    def down_copy(k, j, piece):
        return zw_copy(k, j, piece, even, zw_sem.at[0], me - 2)

    def up_copy(k, j, piece):
        return zw_copy(k, j, piece, even, up_sem, me + 2)

    def z_recv(k, j, piece):
        return zw_copy(k, j, piece, 1 - even, zw_sem.at[0], me)

    def zt_copy(k, j, base):
        spot = wfull.at[j // PARTS, place(behind(base, k), 1 - even, j % PARTS), :]
        return head_copy(spot, spot, zt_sem.at[0, k, j], zt_sem.at[1, k, j], twin)

    def p1_copy(u):
        h, sub = lax.div(u, SUB), lax.rem(u, SUB)
        rows = pl.ds(aligned((1 - parity) * column_rows + sub * unit_rows, unit_rows), unit_rows)
        return seq_copy(
            memb.at[h, rows, :], p1in.at[u], p1_sem.at[0, u], p1_sem.at[1, u], partner
        )

    def z_copy(u):
        return seq_copy(zout.at[u], zin.at[u], z_sem.at[0, u], z_sem.at[1, u], me + 2)

    def y_copy(u, side):
        h, sub = lax.div(u, SUB), lax.rem(u, SUB)
        rows = pl.ds(aligned(side * column_rows + sub * unit_rows, unit_rows), unit_rows)
        return seq_copy(yout.at[u], sin.at[h, rows, :], y_sem.at[0, u], y_sem.at[1, u], partner)

    def rows_of(owner):
        return pl.ds(aligned(owner * own_rows, own_rows), own_rows)

    def row_send(h, to):
        return head_copy(
            fin.at[h, rows_of(to), :],
            exch.at[h, :, block_of(mine)],
            row_sem.at[0, h, to],
            row_sem.at[1, h, mine],
            to,
        )

    def row_recv(h, source):
        return head_copy(
            fin.at[h, rows_of(source), :],
            exch.at[h, :, block_of(source)],
            row_sem.at[0, h, source],
            row_sem.at[1, h, source],
            source,
        )

    def loop(start, stop, body):
        def step(i, carry):
            body(i)
            return carry

        lax.fori_loop(start, stop, step, 0)

    for side in range(2):
        wkv_copy(0, side).start()
    for i in range(tiles):
        tok_copy(i).start()
    for h in range(1, heads):
        for side in range(2):
            wkv_copy(h, side).start()
    for i in range(heads // 2):
        wq_copy(i).start()

    pl.semaphore_signal(barrier, 1, device_id={"seq": partner}, device_id_type=MESH)

    @pl.when(plane > 0)
    def _():
        pl.semaphore_signal(barrier, 1, device_id={"seq": me - 2}, device_id_type=MESH)

    @pl.when(plane < planes - 1)
    def _():
        pl.semaphore_signal(barrier, 1, device_id={"seq": me + 2}, device_id_type=MESH)

    for k in range(1, groups):
        pl.semaphore_signal(
            barrier, 1, device_id={"head": lax.rem(mine + k, groups)}, device_id_type=MESH
        )
    waits = 1 + (groups - 1) + jnp.where(plane > 0, 1, 0) + jnp.where(plane < planes - 1, 1, 0)
    pl.semaphore_wait(barrier, waits)
    for j in range(parts):
        for k in range(1, chips):
            x_send(k, j).start()

    lane = lax.broadcasted_iota(jnp.int32, (heads, rows_all), 1)
    spot = lax.rem(lane, CH)
    rate = rates[...]
    total = -rate
    later = -rate
    step = 1
    while step < CH:
        total = total + jnp.where(spot >= step, pltpu.roll(total, step, 1), 0.0)
        later = later + jnp.where(
            spot < CH - step, pltpu.roll(later, rows_all - step, 1), 0.0
        )
        step *= 2
    later = later + rate
    rowbuf[...] = jnp.zeros_like(rowbuf)
    rowbuf[0:heads, :] = total
    for h in range(heads):
        cum[h] = total[h : h + 1]
        tail[h] = jnp.exp(later[h : h + 1])
        endr[h] = (total + later)[h : h + 1]

    spread = jnp.where(
        lax.div(lax.broadcasted_iota(jnp.int32, (blocks, rows_all), 1), CH)
        == lax.broadcasted_iota(jnp.int32, (blocks, rows_all), 0),
        1.0,
        0.0,
    )
    wide_lane = lax.broadcasted_iota(jnp.int32, (M, rows_all), 1)
    memory_id = lax.broadcasted_iota(jnp.int32, (M, rows_all), 0).astype(F32)

    def place_reads(h):
        named = dot(routing[h].astype(F32), spread)
        share = dot(shares[h], spread, precision=HIGHEST)
        first = named[0:1] == memory_id
        second = named[1:2] == memory_id
        written = jnp.where(first, 1.0, jnp.where(second, 1.0, 0.0))
        mix = jnp.where(first, share[0:1], jnp.where(second, share[1:2], 0.0))
        own = written * endr[h]
        upto = own
        step = CH
        while step < rows_all:
            upto = upto + jnp.where(wide_lane >= step, pltpu.roll(upto, step, 1), 0.0)
            step *= 2
        whole = upto[:, rows_all - 1 : rows_all]
        ei_ref[h] = upto
        e_ref[h] = upto - own
        sh_ref[h] = mix
        wrow[h] = written * jnp.exp(whole - upto) * tail[h]
        prod[h] = jnp.broadcast_to(jnp.exp(whole), (M, HD))
        prod_copy(h).start()


    @pl.when(plane == 0)
    def _():
        zin[...] = jnp.zeros_like(zin)

    def chain_step(u):
        h, sub = lax.div(u, SUB), lax.rem(u, SUB)
        p1_copy(u).wait_recv()

        @pl.when(plane > 0)
        def _():
            z_copy(u).wait_recv()

        start = aligned(parity * column_rows + sub * unit_rows, unit_rows)
        for i in range(unit_rows // HD):
            part = pl.ds(i * HD, HD)
            rows = pl.ds(aligned(start + i * HD, HD), HD)
            m = parity * (M // 2) + sub * (unit_rows // HD) + i
            arrived = zin[u, part, :].astype(F32)
            mine_mem = memb[h, rows, :].astype(F32)
            other_mem = p1in[u, part, :].astype(F32)
            mine_prod = prod[h, pl.ds(m, 1), :]
            other_prod = prodpar[h, pl.ds(m, 1), :]
            lead = parity == 0
            early_mem = jnp.where(lead, mine_mem, other_mem)
            late_mem = jnp.where(lead, other_mem, mine_mem)
            early_prod = jnp.where(lead, mine_prod, other_prod)
            late_prod = jnp.where(lead, other_prod, mine_prod)
            stepped = early_prod * arrived + early_mem
            zout[u, part, :] = (late_prod * stepped + late_mem).astype(BF)
            yout[u, part, :] = jnp.where(lead, stepped, arrived).astype(BF)
            sin[h, rows, :] = jnp.where(lead, arrived, stepped).astype(BF)

        @pl.when(plane < planes - 1)
        def _():
            z_copy(u).start()

        y_copy(u, parity).start()

    clock = [0]

    def due(tick):
        ready = tick - WAIT_TICKS - HOP_TICKS * plane
        return jnp.minimum(jnp.maximum(ready, 0), units)

    def chain_to(tick):
        loop(due(clock[0]), due(tick), chain_step)
        clock[0] = tick

    def service(j):
        for k in range(1, chips):
            x_recv(k, j).wait_recv()
            xt_copy(k, j, mine).start()

        @pl.when(plane > 0)
        def _():
            for k in range(1, chips):
                for piece in range(PIECES):
                    down_copy(k, j, piece).start()

    def rise(first, last):
        @pl.when(plane == planes - 2)
        def _():
            for j in range(first, last):
                for k in range(1, chips):
                    for piece in range(PIECES):
                        up_copy(k, j, piece).start()

    def late_service(h):
        for j in range(h * PARTS, (h + 1) * PARTS):
            for k in range(1, chips):
                for piece in range(PIECES):
                    z_recv(k, j, piece).wait_recv()
                zt_copy(k, j, mine).start()

    served = [0]

    def serve(n):
        while served[0] < min(n, parts):
            service(served[0])
            if served[0] < parts // 2 - 1:
                rise(served[0], served[0] + 1)
            served[0] += 1

    def project(h):
        for side in range(2):
            wkv_copy(h, side).wait()
        if h == 0:
            n = rows_all // 2
            for part in range(2):
                for i in range(tiles // 2):
                    tok_copy(part * tiles // 2 + i).wait()
                rows = slice(part * n, (part + 1) * n)
                both[h % 2, rows, :] = dot(tok[rows, :], wkv[h])
        else:
            both[h % 2] = dot(tok[...], wkv[h])

    def remember(h):
        for i in range(rows_all // HD):
            rows = slice(i * HD, (i + 1) * HD)
            v[h, rows, :] = both[h % 2, rows, HD:].astype(BF)
            wide = both[h % 2, rows, :HD].astype(BF).astype(F32)
            keys = wide * lax.rsqrt(jnp.sum(wide * wide, axis=-1, keepdims=True) + 1e-06)
            turned = jnp.transpose(keys.astype(BF).astype(F32))
            kt[h, :, rows] = turned.astype(BF)
            for m in range(M):
                ks[m * HD : (m + 1) * HD, rows] = (turned * wrow[h, m : m + 1, rows]).astype(BF)
        memb[h] = dot(ks[...], v[h]).astype(BF)

    def give(h):
        for sub in range(SUB):
            p1_copy(h * SUB + sub).start()

    def query(i):
        wq_copy(i).wait()
        pair = dot(tok[...], wq[i]).astype(BF)
        q[2 * i] = pair[:, :HD]
        q[2 * i + 1] = pair[:, HD:]

    place_reads(0)
    project(0)
    own_copy.start()
    for h in range(heads):
        if h + 1 < heads:
            project(h + 1)
            place_reads(h + 1)
        else:
            query(0)
        remember(h)
        give(h)
        if h == 0:
            twin_copy(mine).start()
        prod_copy(h).wait_recv()
        chain_to((h + 1) * SUB)
        serve((h + 1) * parts // (2 * heads))
    for i in range(1, heads // 2):
        query(i)
        chain_to(clock[0] + 1)

    tile_lane = lax.broadcasted_iota(jnp.int32, (CH, TILE), 1)
    tile_row = lax.broadcasted_iota(jnp.int32, (CH, TILE), 0)
    columns = jnp.transpose(rowbuf[...])
    for h in range(heads):
        cb[h] = jnp.broadcast_to(columns[:, h : h + 1], (rows_all, HD))

    def tables(h):
        upto, before, mix, decay = ei_ref[h], e_ref[h], sh_ref[h], tail[h]
        written = jnp.where(mix > 0.0, 1.0, 0.0)
        amount = jnp.sum(mix, axis=0, keepdims=True)
        reads = mix * jnp.exp(before)
        for b in range(blocks):
            at = slice(b * CH, b * CH + 1)
            n = (b // per_tile + 1) * TILE
            coef[h, b] = jnp.broadcast_to(reads[:, at], (M, HD))
            gap = jnp.minimum(before[:, at] - upto[:, :n], 0.0)
            pull = jnp.sum(mix[:, at] * written[:, :n] * jnp.exp(gap), axis=0, keepdims=True)
            position = lax.broadcasted_iota(jnp.int32, (1, n), 1)
            cr[h, b : b + 1, :n] = jnp.where(
                position < b * CH,
                pull * decay[:, :n],
                jnp.where(position < (b + 1) * CH, amount[:, :n], 0.0),
            )

    def attend(h, g):
        rows = slice(g * TILE, (g + 1) * TILE)
        query_rows = q[h, rows, :]
        growth = jnp.exp(cb[h, rows, :])
        acc = jnp.zeros((TILE, HD), F32)
        for t in range(g):
            cols = slice(t * TILE, (t + 1) * TILE)
            scores = dot(query_rows, kt[h, :, cols])
            pulls = [
                (
                    scores[i * CH : (i + 1) * CH]
                    * cr[h, g * per_tile + i : g * per_tile + i + 1, cols]
                ).astype(BF)
                for i in range(per_tile)
            ]
            acc = acc + dot(jnp.concatenate(pulls, axis=0), v[h, cols, :])
        scores = dot(query_rows, kt[h, :, rows])
        pulls = []
        for i in range(per_tile):
            b = g * per_tile + i
            own = cb[h, b * CH : (b + 1) * CH, :]
            col = jnp.concatenate([own] * (TILE // HD), axis=1)
            inside = lax.div(tile_lane, CH) == i
            gap = col - jnp.where(inside, cum[h, :, rows], 0.0)
            factor = jnp.exp(jnp.minimum(gap, 0.0)) * cr[h, b : b + 1, rows]
            factor = jnp.where(tile_lane <= tile_row + i * CH, factor, 0.0)
            pulls.append((scores[i * CH : (i + 1) * CH] * factor).astype(BF))
        near = dot(jnp.concatenate(pulls, axis=0), v[h, rows, :])
        intra[h, rows, :] = acc * growth + near
        grown = query_rows.astype(F32) * growth
        for i in range(per_tile):
            b = g * per_tile + i
            piece = grown[i * CH : (i + 1) * CH]
            for m in range(M):
                qs[h, b * CH : (b + 1) * CH, m * HD : (m + 1) * HD] = (
                    piece * coef[h, b, m : m + 1, :]
                ).astype(BF)

    for h in range(heads):
        tables(h)
        for g in range(tiles):
            attend(h, g)
            if g % 2 == 1:
                chain_to(clock[0] + 1)
        serve(parts // 2 + (h + 1) * parts // (2 * heads))

    def finish(h):
        for sub in range(SUB):
            y_copy(h * SUB + sub, 1 - parity).wait_recv()
        for k in range(1, chips + 1):
            to = lax.rem(chip + k, chips)
            n = 2 * own_rows
            rows = pl.ds(aligned(to * n, n), n)
            whole = intra[h, rows, :] + dot(qs[h, rows, :], sin[h])
            scale = lax.rsqrt(jnp.mean(whole * whole, axis=-1, keepdims=True) + 1e-06)
            fin[h, rows, :] = (whole * scale * gain[h]).astype(BF)
            if k < chips:
                row_send(h, 2 * to + core).start()
                row_send(h, 2 * to + 1 - core).start()
            else:
                row_send(h, twin).start()
        exch[h, :, block_of(mine)] = fin[h, rows_of(mine), :]

    def others(body):
        for k in range(1, chips):
            to = lax.rem(chip + k, chips)
            body(2 * to + core)
            body(2 * to + 1 - core)
        body(twin)

    def emit(h):
        others(lambda source: row_recv(h, source).wait_recv())
        for j in range(h * PARTS, (h + 1) * PARTS):
            for k in range(1, chips):
                xt_copy(k, j, twin).wait_recv()
                zt_copy(k, j, twin).wait_recv()
        for part in range(depth // 512):
            cols = slice(part * 512, (part + 1) * 512)
            more = dot(exch[h], wfull[h, :, cols])
            if h > 0:
                more = oacc[:, cols] + more
            if h == heads - 1:
                out[:, cols] = more.astype(BF)
            else:
                oacc[:, cols] = more

    for h in range(heads):
        ahead = min(h + 2, heads) * SUB if h < heads - 2 else units
        chain_to(max(clock[0], WAIT_TICKS + HOP_TICKS * (planes - 1) + ahead))
        if h == 0:
            rise(max(parts // 2 - 1, 0), parts // 2 + 1)
        if h == max(heads - 2, 0):
            rise(parts // 2 + 1, parts)
        finish(h)
        late_service(h)
        if h == 0:
            own_copy.wait()
            twin_copy(twin).wait_recv()
        if h > 0:
            emit(h - 1)
    emit(heads - 1)

    for h in range(heads):
        prod_copy(h).wait_send()
    twin_copy(mine).wait_send()
    for j in range(parts):
        for k in range(1, chips):
            x_send(k, j).wait_send()
            xt_copy(k, j, mine).wait_send()
            zt_copy(k, j, mine).wait_send()

    @pl.when(plane > 0)
    def _():
        for j in range(parts):
            for k in range(1, chips):
                for piece in range(PIECES):
                    down_copy(k, j, piece).wait_send()

    @pl.when(plane == planes - 2)
    def _():
        for j in range(parts):
            for k in range(1, chips):
                for piece in range(PIECES):
                    up_copy(k, j, piece).wait_send()

    for h in range(heads):
        others(lambda to: row_send(h, to).wait_send())

    def drain_units(u):
        p1_copy(u).wait_send()
        y_copy(u, parity).wait_send()

        @pl.when(plane < planes - 1)
        def _():
            z_copy(u).wait_send()

    loop(0, units, drain_units)


def per_device(
    tokens, w_query, w_key, w_value, w_out, norm_gain, forget_rate, routing, memory_blend_share
):
    rows, depth = tokens.shape
    width = w_query.shape[1]
    heads = width // HD
    blocks = rows // CH
    groups, size = lax.axis_size("head"), lax.axis_size("seq")
    assert size % 4 == 0 and groups % 2 == 0 and heads % 2 == 0 and rows % TILE == 0
    chips = groups // 2
    own_rows = rows // groups
    units = heads * SUB
    unit_rows = M * HD // 2 // SUB
    parts = heads * PARTS
    vmem = pl.BlockSpec(memory_space=VMEM)
    hbm = pl.BlockSpec(memory_space=pl.ANY)
    return pl.pallas_call(
        layer_kernel,
        out_shape=jax.ShapeDtypeStruct((own_rows, depth), BF),
        in_specs=[vmem] * 4 + [hbm] * 5,
        out_specs=vmem,
        scratch_shapes=[
            VMEM((rows, depth), BF),
            VMEM((heads, depth, 2 * HD), BF),
            VMEM((heads // 2, depth, 2 * HD), BF),
            VMEM((2, rows, 2 * HD), F32),
            VMEM((heads, rows, HD), BF),
            VMEM((heads, HD, rows), BF),
            VMEM((heads, rows, HD), BF),
            VMEM((M * HD, rows), BF),
            VMEM((heads, M * HD, HD), BF),
            VMEM((units, unit_rows, HD), BF),
            VMEM((units, unit_rows, HD), BF),
            VMEM((units, unit_rows, HD), BF),
            VMEM((units, unit_rows, HD), BF),
            VMEM((heads, M * HD, HD), BF),
            VMEM((8, rows), F32),
            VMEM((heads, 1, rows), F32),
            VMEM((heads, 1, rows), F32),
            VMEM((heads, 1, rows), F32),
            VMEM((heads, M, rows), F32),
            VMEM((heads, M, rows), F32),
            VMEM((heads, M, rows), F32),
            VMEM((heads, M, rows), F32),
            VMEM((heads, M, HD), F32),
            VMEM((heads, M, HD), F32),
            VMEM((heads, blocks, M, HD), F32),
            VMEM((heads, blocks, rows), F32),
            VMEM((heads, rows, HD), F32),
            VMEM((heads, rows, M * HD), BF),
            VMEM((heads, rows, HD), F32),
            VMEM((heads, rows, HD), BF),
            VMEM((heads, own_rows, groups * HD), BF),
            VMEM((heads, groups * HD, depth), BF),
            VMEM((own_rows, depth), F32),
            DMA((rows // TILE,)),
            DMA((heads, 2)),
            DMA((heads // 2,)),
            DMA,
            DMA((2, heads)),
            DMA((2, units)),
            DMA((2, units)),
            DMA((2, units)),
            DMA((2, heads, groups)),
            DMA((2,)),
            DMA((2, chips, parts)),
            DMA((2, chips, parts)),
            DMA((2, chips, parts, PIECES)),
            DMA((chips, parts, PIECES)),
            DMA((2, chips, parts)),
        ],
        compiler_params=pltpu.CompilerParams(
            collective_id=0, has_side_effects=True, vmem_limit_bytes=LIMIT
        ),
        name="layer",
    )(
        forget_rate.T,
        jnp.transpose(routing, (1, 2, 0)),
        jnp.transpose(memory_blend_share, (1, 2, 0)),
        norm_gain.reshape(heads, 1, HD),
        tokens,
        w_query,
        w_key,
        w_value,
        w_out.reshape(heads, HD, depth),
    )


def solution(mesh):
    placed = (
        P("seq", None),
        P(None, "head"),
        P(None, "head"),
        P(None, "head"),
        P("head", None),
        P("head"),
        P("seq", "head"),
        P("seq", "head", None),
        P("seq", "head", None),
    )
    return jax.shard_map(
        per_device, mesh=mesh, in_specs=placed, out_specs=P(("seq", "head"), None), check_vma=False
    )
```

time: 65.8 us -> 59.3 us (0.901)
  the two profiles are of different devices: /device:TPU:1 before, /device:TPU:25 now
where the time goes in v2:
time: 59.3 us; the launch traced here: 59.1 us
  Pallas kernels  56.8 us (96%)
  local copies, waits for them, and re-layouts  2.3 us (4%)
    pallas_call x1, Pallas kernels, per_device(): pl.pallas_call(layer_kernel, out_shape=jax.ShapeDtypeStruct((own_rows, de...  56.8 us
    unnamed x1, local copies, waits for them, and re-layouts  2.3 us

profile of v2, /device:TPU:25, one launch (start us, length us, event | category | flops | bytes accessed | tf_op | source)
XLA Modules:
  0.0 59.1 jit_solution(17155638559101280928)
XLA Ops:
  0.0 56.8 %layer.1 = bf16[256,2048]{1,0:T(8,128)(2,1)} custom-call(f32[4,1024]{1,0:T(4,128)} %bitcast.6, s32[4,2,16]{2,1,0:T(2,128)} %bitcast.7, f32[4,2,16]{2,1,0:T(2,128)} %bitcast.8, f32[4,1,128]{2,1,0:T(1,128)} %bitcast.9, bf16[1024,2048]{1,0:T(8,128)(2,1)} %tokens.1, bf16[2048,512]{1,0:T(8,128)(2,1)} %w_query.1, bf16[2048,512]{1,0:T(8,128)(2,1)} %w_key.1, ...), custom_call_target="tpu_custom_call" | custom-call | tf_op jit(solution)/shard_map/layer/pallas_call | solution.py:663
  56.8 2.3 %copy.11 = bf16[256,2048]{1,0:T(8,128)(2,1)} copy(bf16[256,2048]{1,0:T(8,128)(2,1)} %layer.1) | data formatting | bytes 2097152
